TPU v7x, 256 devices: a whole 4x4x8 slice. The times are simulated.
256 devices in a mesh: dp: 8 (over x, z_hi), pipe: 4 (over z_lo), expert: 8 (over y, core).
Axes of the slice: x: 4, y: 4, z: 8 (z_hi: 2, z_lo: 4; z = z_hi * 4 + z_lo), core: 2. Of those that a mesh axis runs over, the one named last changes fastest.
Arguments:
- tokens: bfloat16 [8192, 2048], P(('dp', 'expert')), may hold values from -6 to 6
- cotangent: bfloat16 [8192, 2048], P(('dp', 'expert')), may hold values from -6 to 6
- owner_ids: int32 [4, 8192, 4], P('pipe', ('dp', 'expert')), may hold values from 0 to 63, all different within a row; in each aligned block of 32 rows (0 to 31, 32 to 63, ..., all dimensions but the last counted through in order) at most 3 rows name the same one
- gate_weights: bfloat16 [4, 8192, 4], P('pipe', ('dp', 'expert')), may hold values from 0.049804688 to 0.25
- norm_gain: float32 [4, 2048], P('pipe'), may hold values from 0.5 to 1.5
- w_gate: bfloat16 [4, 64, 2048, 384], P('pipe', ('dp', 'expert')), may hold values from -0.125 to 0.125
- w_up: bfloat16 [4, 64, 2048, 384], P('pipe', ('dp', 'expert')), may hold values from -0.125 to 0.125
- w_down: bfloat16 [4, 64, 384, 2048], P('pipe', ('dp', 'expert')), may hold values from -0.3125 to 0.3125
Outputs:
- segment_out: bfloat16 [4, 8192, 2048], P('pipe', ('dp', 'expert'))
- segment_grad: bfloat16 [4, 8192, 2048], P('pipe', ('dp', 'expert'))
- gain_grad: float32 [4, 2048], P('pipe')
Inputs may be any that keep to these rules, and one draw needn't show every extreme that they name: `owner_ids`: each row names 4 different owners. In each aligned block of 32 rows (layers in order, then tokens) no owner is named by more than 3 rows, and that bound is reached.
All inputs are finite; a program needn't handle non-finite values.
Results may differ from a plain program's by a relative error of at most 0.014.
Values may be sent and summed in bfloat16 or wider, within the bound.
A program may use at most 128 MiB of HBM per device.

v0:
```python
import jax
import jax.numpy as jnp
from jax import lax
from jax.sharding import PartitionSpec as P

MICRO = 4
epsilon = 1e-06


def from_behind(value, axis, steps):
    count = lax.axis_size(axis)
    leading, last = (max(0, -steps), min(count, count - steps))
    return lax.ppermute(value, axis, [(source, source + steps) for source in range(leading, last)])


def inverse_rms(values):
    return lax.rsqrt(jnp.mean(values * values, axis=-1, keepdims=True) + epsilon)


def contract_last(left, right):
    return lax.dot_general(
        left, right, (((1,), (1,)), ((), ())), preferred_element_type=jnp.float32
    )


def route_tables(ids_part, owners, capacity):
    owner_range = jnp.arange(owners, dtype=jnp.int32)
    onehot = (ids_part[:, :, None] == owner_range[None, None, :]).astype(jnp.int32)
    member = jnp.sum(onehot, axis=1)
    position = jnp.cumsum(member, axis=0) - member
    slot_range = jnp.arange(capacity, dtype=jnp.int32)
    placed = (position[:, :, None] == slot_range[None, None, :]) & (member[:, :, None] > 0)
    placing = jnp.transpose(placed, (1, 2, 0)).astype(jnp.bfloat16)
    return (onehot.astype(jnp.float32), placing)


def gate_slots(onehot, gates_part, placing, experts_here):
    gate_pairs = gates_part.astype(jnp.float32).reshape(gates_part.shape[0], -1, experts_here)
    chosen = jnp.einsum("rjo,rjc->roc", onehot, gate_pairs)
    return jnp.einsum("okr,roc->okc", placing.astype(jnp.float32), chosen).astype(jnp.bfloat16)


def send_rows(row_block, pair_block):
    got_rows, got_pairs = (
        lax.all_to_all(row_block, ("dp", "expert"), split_axis=0, concat_axis=0, tiled=True),
        lax.all_to_all(pair_block, ("dp", "expert"), split_axis=0, concat_axis=0, tiled=True),
    )
    return (got_rows, got_pairs)


def return_rows(row_block):
    return lax.all_to_all(row_block, ("dp", "expert"), split_axis=0, concat_axis=0, tiled=True)


def send_grads(row_block):
    return lax.all_to_all(row_block, ("dp", "expert"), split_axis=0, concat_axis=0, tiled=True)


def return_grads(row_block):
    return lax.all_to_all(row_block, ("dp", "expert"), split_axis=0, concat_axis=0, tiled=True)


def expert_forward(flat_rows, flat_pairs, joint_mats, down_mats):
    hidden_width = down_mats.shape[1]
    joint_pre = jnp.dot(flat_rows, joint_mats[0], preferred_element_type=jnp.float32)
    gate_pre = joint_pre[:, :hidden_width]
    up_pre = joint_pre[:, hidden_width:]
    hidden = (jax.nn.silu(gate_pre) * up_pre).astype(jnp.bfloat16)
    projected = jnp.dot(hidden, down_mats[0], preferred_element_type=jnp.float32)
    term = flat_pairs.astype(jnp.float32) * projected
    kept_both = [joint_pre]
    return (term.astype(jnp.bfloat16), jnp.stack(kept_both))


def expert_backward(grad_rows, flat_pairs, joint_keep, joint_mats, down_mats):
    hidden_width = down_mats.shape[1]
    q_vals = contract_last(grad_rows, down_mats[0])
    gate_pre = joint_keep[0][:, :hidden_width]
    up_pre = joint_keep[0][:, hidden_width:]
    sigma = jax.nn.sigmoid(gate_pre)
    weight = flat_pairs.astype(jnp.float32)
    d_gate = (q_vals * weight * up_pre * sigma * (1.0 + gate_pre * (1.0 - sigma))).astype(
        jnp.bfloat16
    )
    d_up = (q_vals * weight * gate_pre * sigma).astype(jnp.bfloat16)
    joint_grad = jnp.concatenate([d_gate, d_up], axis=1)
    term = contract_last(joint_grad, joint_mats[0])
    return term.astype(jnp.bfloat16)


def body(tokens, cotangent, owner_ids, gate_weights, norm_gain, w_gate, w_up, w_down):
    segments = lax.axis_size("pipe")
    segment_index = lax.axis_index("pipe")
    owners = lax.axis_size("dp") * lax.axis_size("expert")
    tok_rows = tokens.shape[0]
    width = tokens.shape[1]
    micro_rows = tok_rows // MICRO
    route_count = owner_ids.shape[2]
    capacity = max(2, (5 * micro_rows * route_count + 4 * owners - 1) // (4 * owners))
    slot_count = owners * capacity
    gain_row = norm_gain[0]
    joint_mats = jnp.concatenate([w_gate[0], w_up[0]], axis=2)
    down_mats = w_down[0]
    layer_ids = owner_ids[0]
    layer_gates = gate_weights[0]
    experts_here = joint_mats.shape[0]
    joint_width = joint_mats.shape[2]

    def skip_forward(operands):
        return (
            jnp.zeros((slot_count, width), jnp.bfloat16),
            jnp.zeros((experts_here, slot_count, joint_width), jnp.float32),
        )

    def run_forward(operands):
        return expert_forward(operands[0], operands[1], joint_mats, down_mats)

    def skip_backward(operands):
        return jnp.zeros((slot_count, width), jnp.bfloat16)

    def run_backward(operands):
        return expert_backward(operands[0], operands[1], operands[2], joint_mats, down_mats)

    def timing(micro):
        is_valid = (micro >= 0) & (micro < MICRO)
        slot_pick = jnp.where(is_valid, micro, MICRO)
        start_row = jnp.clip(micro, 0, MICRO - 1) * micro_rows
        return (is_valid, slot_pick, start_row)

    layer_outs = jnp.zeros((MICRO + 1, micro_rows, width), jnp.bfloat16)
    layer_ins = jnp.zeros((MICRO + 1, micro_rows, width), jnp.bfloat16)
    kept_joint = jnp.zeros((MICRO + 1, experts_here, slot_count, joint_width), jnp.float32)
    kept_pairs = jnp.zeros((MICRO + 1, slot_count, experts_here), jnp.bfloat16)
    grad_outs = jnp.zeros((MICRO + 1, micro_rows, width), jnp.bfloat16)
    gain_sum = jnp.zeros((width,), jnp.float32)
    ticks = MICRO + segments - 1
    incoming = jnp.zeros((micro_rows, width), jnp.bfloat16)
    for tick_num in range(ticks):
        forward_is_valid, forward_slot_pick, forward_start_row = timing(tick_num - segment_index)
        forward_own_part = lax.dynamic_slice_in_dim(tokens, forward_start_row, micro_rows, 0)
        forward_layer_in = jnp.where(segment_index == 0, forward_own_part, incoming)
        forward_ids_part = lax.dynamic_slice_in_dim(layer_ids, forward_start_row, micro_rows, 0)
        gates_part = lax.dynamic_slice_in_dim(layer_gates, forward_start_row, micro_rows, 0)
        forward_x_float = forward_layer_in.astype(jnp.float32)
        forward_scale = inverse_rms(forward_x_float)
        normed = (forward_x_float * forward_scale * gain_row).astype(jnp.bfloat16)
        forward_onehot, forward_placing = route_tables(forward_ids_part, owners, capacity)
        row_block = jnp.einsum(
            "okr,rd->okd", forward_placing, normed, preferred_element_type=jnp.float32
        ).astype(jnp.bfloat16)
        pair_block = gate_slots(forward_onehot, gates_part, forward_placing, experts_here)
        f_valid, f_pick, layer_in, x_float, f_placing, row_block, pair_block = (
            forward_is_valid,
            forward_slot_pick,
            forward_layer_in,
            forward_x_float,
            forward_placing,
            row_block,
            pair_block,
        )
        got_rows, got_pairs = send_rows(row_block, pair_block)
        flat_rows = got_rows.reshape(slot_count, width)
        flat_pairs = got_pairs.reshape(slot_count, experts_here)
        result, joint_pre = lax.cond(f_valid, run_forward, skip_forward, (flat_rows, flat_pairs))
        returned = return_rows(result.reshape(owners, capacity, width))
        branch = jnp.einsum("okr,okd->rd", f_placing, returned, preferred_element_type=jnp.float32)
        layer_out = (x_float + branch).astype(jnp.bfloat16)
        layer_outs = lax.dynamic_update_index_in_dim(layer_outs, layer_out, f_pick, 0)
        layer_ins = lax.dynamic_update_index_in_dim(layer_ins, layer_in, f_pick, 0)
        kept_joint = lax.dynamic_update_index_in_dim(kept_joint, joint_pre, f_pick, 0)
        kept_pairs = lax.dynamic_update_index_in_dim(kept_pairs, flat_pairs, f_pick, 0)
        if tick_num + 1 < ticks:
            incoming = from_behind(layer_out, "pipe", 1)
    incoming = jnp.zeros((micro_rows, width), jnp.bfloat16)
    for tick_num in range(ticks):
        backward_is_valid, backward_slot_pick, backward_start_row = timing(
            tick_num - (segments - 1 - segment_index)
        )
        own_part = lax.dynamic_slice_in_dim(cotangent, backward_start_row, micro_rows, 0)
        backward_grad_in = jnp.where(segment_index == segments - 1, own_part, incoming)
        ids_part = lax.dynamic_slice_in_dim(layer_ids, backward_start_row, micro_rows, 0)
        backward_layer_in = lax.dynamic_index_in_dim(
            layer_ins, backward_slot_pick, 0, keepdims=False
        )
        backward_x_float = backward_layer_in.astype(jnp.float32)
        backward_scale = inverse_rms(backward_x_float)
        onehot, backward_placing = route_tables(ids_part, owners, capacity)
        grad_block = jnp.einsum(
            "okr,rd->okd", backward_placing, backward_grad_in, preferred_element_type=jnp.float32
        ).astype(jnp.bfloat16)
        b_valid, b_pick, grad_in, bx_float, b_scale, b_placing, grad_block = (
            backward_is_valid,
            backward_slot_pick,
            backward_grad_in,
            backward_x_float,
            backward_scale,
            backward_placing,
            grad_block,
        )
        got_grads = send_grads(grad_block).reshape(slot_count, width)
        joint_keep = lax.dynamic_index_in_dim(kept_joint, b_pick, 0, keepdims=False)
        pair_keep = lax.dynamic_index_in_dim(kept_pairs, b_pick, 0, keepdims=False)
        owner_grad = lax.cond(
            b_valid, run_backward, skip_backward, (got_grads, pair_keep, joint_keep)
        )
        returned = return_grads(owner_grad.reshape(owners, capacity, width))
        normed_grad = jnp.einsum(
            "okr,okd->rd", b_placing, returned, preferred_element_type=jnp.float32
        )
        weighted = gain_row * normed_grad
        grad_x = (
            grad_in.astype(jnp.float32)
            + b_scale * weighted
            - bx_float
            * b_scale
            * b_scale
            * b_scale
            * jnp.mean(weighted * bx_float, axis=-1, keepdims=True)
        )
        gain_term = jnp.where(b_valid, jnp.sum(normed_grad * bx_float * b_scale, axis=0), 0.0)
        grad_bf, gain_term = (grad_x.astype(jnp.bfloat16), gain_term)
        grad_outs = lax.dynamic_update_index_in_dim(grad_outs, grad_bf, b_pick, 0)
        gain_sum = gain_sum + gain_term
        if tick_num + 1 < ticks:
            incoming = from_behind(grad_bf, "pipe", -1)
    gain_grad = lax.psum(gain_sum, ("dp", "expert"))
    segment_out = layer_outs[:MICRO].reshape(1, tok_rows, width)
    segment_grad = grad_outs[:MICRO].reshape(1, tok_rows, width)
    return (segment_out, segment_grad, gain_grad.reshape(1, width))


def solution(mesh):
    in_specs = (
        P(("dp", "expert"), None),
        P(("dp", "expert"), None),
        P("pipe", ("dp", "expert"), None),
        P("pipe", ("dp", "expert"), None),
        P("pipe", None),
        P("pipe", ("dp", "expert"), None, None),
        P("pipe", ("dp", "expert"), None, None),
        P("pipe", ("dp", "expert"), None, None),
    )
    out_specs = (
        P("pipe", ("dp", "expert"), None),
        P("pipe", ("dp", "expert"), None),
        P("pipe", None),
    )
    return jax.shard_map(body, mesh=mesh, in_specs=in_specs, out_specs=out_specs, check_vma=False)
```

profile of v0, /device:TPU:1, one launch (start us, length us, event | category | flops | bytes accessed | tf_op | source)
XLA Modules:
  0.0 1507.8 jit_solution(17595029229092546663)
XLA Ops:
  5.5 15.6 %all-to-all-start = ((bf16[64,3,1]{1,2,0:T(2,128)(2,1)}), bf16[64,3,1]{1,2,0:T(2,128)(2,1)S(1)}, u32[]{:S(2)}, u32[]{:S(2)}) async-start(bf16[64,3,1]{1,2,0:T(2,128)(2,1)} %copy.214), calls=%async_computation | async-start | bytes 65536 | tf_op jit(solution)/shard_map/all_to_all | solution.py:46
  25.2 7.5 all-to-all-done
  40.4 25.5 %all-to-all-done.1 = bf16[64,3,2048]{2,1,0:T(4,128)(2,1)} async-done(((bf16[64,3,2048]{2,1,0:T(4,128)(2,1)}), bf16[64,3,2048]{2,1,0:T(4,128)(2,1)}, u32[]{:S(2)}, u32[]{:S(2)}) %all-to-all-start.1) | async-done | bytes 786464 | tf_op jit(solution)/shard_map/all_to_all | solution.py:45
  65.9 9.1 conditional.14
  84.8 18.1 %all-to-all-done.2 = bf16[64,3,2048]{2,1,0:T(4,128)(2,1)} async-done(((bf16[64,3,2048]{2,1,0:T(4,128)(2,1)}), bf16[64,3,2048]{2,1,0:T(4,128)(2,1)}, u32[]{:S(2)}, u32[]{:S(2)}) %all-to-all-start.2) | async-done | bytes 786464 | tf_op jit(solution)/shard_map/all_to_all | solution.py:52
  109.9 7.3 collective-permute-start
  122.4 14.5 all-to-all-start.4
  136.9 28.5 %all-to-all-done.4 = bf16[64,3,2048]{2,1,0:T(4,128)(2,1)} async-done(((bf16[64,3,2048]{2,1,0:T(4,128)(2,1)}), bf16[64,3,2048]{2,1,0:T(4,128)(2,1)}, u32[]{:S(2)}, u32[]{:S(2)}) %all-to-all-start.4) | async-done | bytes 786464 | tf_op jit(solution)/shard_map/all_to_all | solution.py:45
  165.4 9.3 conditional.15
  184.1 18.4 %all-to-all-done.5 = bf16[64,3,2048]{2,1,0:T(4,128)(2,1)} async-done(((bf16[64,3,2048]{2,1,0:T(4,128)(2,1)}), bf16[64,3,2048]{2,1,0:T(4,128)(2,1)}, u32[]{:S(2)}, u32[]{:S(2)}) %all-to-all-start.5) | async-done | bytes 786464 | tf_op jit(solution)/shard_map/all_to_all | solution.py:52
  205.4 17.4 %collective-permute-start.1 = (bf16[32,2048]{1,0:T(8,128)(2,1)S(1)}, bf16[32,2048]{1,0:T(8,128)(2,1)S(1)}, u32[]{:S(2)}, u32[]{:S(2)}) collective-permute-start(bf16[32,2048]{1,0:T(8,128)(2,1)S(1)} %get-tuple-element.841), channel_id=1, source_target_pairs={{0,8},{8,16},{16,24},{1,9},{9,17},{17,25},{2,10},{10,18},{18,26},{... | collective-permute-start | bytes 393224 | tf_op jit(solution)/shard_map/ppermute | solution.py:13
  233.7 7.2 all-to-all-done.6
  240.8 5.9 all-to-all-start.7
  246.7 28.6 %all-to-all-done.7 = bf16[64,3,2048]{2,1,0:T(4,128)(2,1)} async-done(((bf16[64,3,2048]{2,1,0:T(4,128)(2,1)}), bf16[64,3,2048]{2,1,0:T(4,128)(2,1)}, u32[]{:S(2)}, u32[]{:S(2)}) %all-to-all-start.7) | async-done | bytes 786464 | tf_op jit(solution)/shard_map/all_to_all | solution.py:45
  275.3 9.1 conditional.16
  287.7 9.0 all-to-all-start.8
  298.6 20.2 %all-to-all-done.8 = bf16[64,3,2048]{2,1,0:T(4,128)(2,1)} async-done(((bf16[64,3,2048]{2,1,0:T(4,128)(2,1)}), bf16[64,3,2048]{2,1,0:T(4,128)(2,1)}, u32[]{:S(2)}, u32[]{:S(2)}) %all-to-all-start.8) | async-done | bytes 786464 | tf_op jit(solution)/shard_map/all_to_all | solution.py:52
  324.2 9.3 all-to-all-start.9
  338.0 7.1 all-to-all-done.9
  350.9 26.9 %all-to-all-done.10 = bf16[64,3,2048]{2,1,0:T(4,128)(2,1)} async-done(((bf16[64,3,2048]{2,1,0:T(4,128)(2,1)}), bf16[64,3,2048]{2,1,0:T(4,128)(2,1)}, u32[]{:S(2)}, u32[]{:S(2)}) %all-to-all-start.10) | async-done | bytes 786464 | tf_op jit(solution)/shard_map/all_to_all | solution.py:45
  377.8 9.1 conditional.17
  390.2 9.2 all-to-all-start.11
  399.7 21.5 %all-to-all-done.11 = bf16[64,3,2048]{2,1,0:T(4,128)(2,1)} async-done(((bf16[64,3,2048]{2,1,0:T(4,128)(2,1)}), bf16[64,3,2048]{2,1,0:T(4,128)(2,1)}, u32[]{:S(2)}, u32[]{:S(2)}) %all-to-all-start.11) | async-done | bytes 786464 | tf_op jit(solution)/shard_map/all_to_all | solution.py:52
  426.2 9.1 all-to-all-start.12
  439.9 7.1 all-to-all-done.12
  452.8 21.8 %all-to-all-done.13 = bf16[64,3,2048]{2,1,0:T(4,128)(2,1)} async-done(((bf16[64,3,2048]{2,1,0:T(4,128)(2,1)}), bf16[64,3,2048]{2,1,0:T(4,128)(2,1)}, u32[]{:S(2)}, u32[]{:S(2)}) %all-to-all-start.13) | async-done | bytes 786464 | tf_op jit(solution)/shard_map/all_to_all | solution.py:45
  486.5 24.1 %all-to-all-done.14 = bf16[64,3,2048]{2,1,0:T(4,128)(2,1)} async-done(((bf16[64,3,2048]{2,1,0:T(4,128)(2,1)}), bf16[64,3,2048]{2,1,0:T(4,128)(2,1)}, u32[]{:S(2)}, u32[]{:S(2)}) %all-to-all-start.14) | async-done | bytes 786464 | tf_op jit(solution)/shard_map/all_to_all | solution.py:52
  517.5 7.1 all-to-all-start.15
  529.1 7.2 all-to-all-done.15
  542.1 22.4 %all-to-all-done.16 = bf16[64,3,2048]{2,1,0:T(4,128)(2,1)} async-done(((bf16[64,3,2048]{2,1,0:T(4,128)(2,1)}), bf16[64,3,2048]{2,1,0:T(4,128)(2,1)}, u32[]{:S(2)}, u32[]{:S(2)}) %all-to-all-start.16) | async-done | bytes 786464 | tf_op jit(solution)/shard_map/all_to_all | solution.py:45
  569.6 9.2 all-to-all-start.17
  580.6 26.7 %all-to-all-done.17 = bf16[64,3,2048]{2,1,0:T(4,128)(2,1)} async-done(((bf16[64,3,2048]{2,1,0:T(4,128)(2,1)}), bf16[64,3,2048]{2,1,0:T(4,128)(2,1)}, u32[]{:S(2)}, u32[]{:S(2)}) %all-to-all-start.17) | async-done | bytes 786464 | tf_op jit(solution)/shard_map/all_to_all | solution.py:52
  612.5 7.5 all-to-all-start.18
  624.5 7.1 all-to-all-done.18
  642.5 23.4 %all-to-all-done.19 = bf16[64,3,2048]{2,1,0:T(4,128)(2,1)} async-done(((bf16[64,3,2048]{2,1,0:T(4,128)(2,1)}), bf16[64,3,2048]{2,1,0:T(4,128)(2,1)}, u32[]{:S(2)}, u32[]{:S(2)}) %all-to-all-start.19) | async-done | bytes 786464 | tf_op jit(solution)/shard_map/all_to_all | solution.py:45
  701.7 20.6 %all-to-all-done.22 = bf16[64,3,2048]{2,1,0:T(4,128)(2,1)} async-done(((bf16[64,3,2048]{2,1,0:T(4,128)(2,1)}), bf16[64,3,2048]{2,1,0:T(4,128)(2,1)}, u32[]{:S(2)}, u32[]{:S(2)}) %all-to-all-start.22) | async-done | bytes 786464 | tf_op jit(solution)/shard_map/all_to_all | solution.py:60
  728.1 14.4 collective-permute-done.6
  750.4 28.5 %all-to-all-done.23 = bf16[64,3,2048]{2,1,0:T(4,128)(2,1)} async-done(((bf16[64,3,2048]{2,1,0:T(4,128)(2,1)}), bf16[64,3,2048]{2,1,0:T(4,128)(2,1)}, u32[]{:S(2)}, u32[]{:S(2)}) %all-to-all-start.23) | async-done | bytes 786464 | tf_op jit(solution)/shard_map/all_to_all | solution.py:56
  788.4 19.0 %all-to-all-done.24 = bf16[64,3,2048]{2,1,0:T(4,128)(2,1)} async-done(((bf16[64,3,2048]{2,1,0:T(4,128)(2,1)}), bf16[64,3,2048]{2,1,0:T(4,128)(2,1)}, u32[]{:S(2)}, u32[]{:S(2)}) %all-to-all-start.24) | async-done | bytes 786464 | tf_op jit(solution)/shard_map/all_to_all | solution.py:60
  812.8 11.5 collective-permute-done.7
  827.4 12.2 all-to-all-start.25
  839.6 28.5 %all-to-all-done.25 = bf16[64,3,2048]{2,1,0:T(4,128)(2,1)} async-done(((bf16[64,3,2048]{2,1,0:T(4,128)(2,1)}), bf16[64,3,2048]{2,1,0:T(4,128)(2,1)}, u32[]{:S(2)}, u32[]{:S(2)}) %all-to-all-start.25) | async-done | bytes 786464 | tf_op jit(solution)/shard_map/all_to_all | solution.py:56
  877.8 19.0 %all-to-all-done.26 = bf16[64,3,2048]{2,1,0:T(4,128)(2,1)} async-done(((bf16[64,3,2048]{2,1,0:T(4,128)(2,1)}), bf16[64,3,2048]{2,1,0:T(4,128)(2,1)}, u32[]{:S(2)}, u32[]{:S(2)}) %all-to-all-start.26) | async-done | bytes 786464 | tf_op jit(solution)/shard_map/all_to_all | solution.py:60
  902.2 17.1 %collective-permute-done.8 = bf16[32,2048]{1,0:T(8,128)(2,1)S(1)} collective-permute-done((bf16[32,2048]{1,0:T(8,128)(2,1)S(1)}, bf16[32,2048]{1,0:T(8,128)(2,1)S(1)}, u32[]{:S(2)}, u32[]{:S(2)}) %collective-permute-start.8) | collective-permute-done | bytes 131104 | tf_op jit(solution)/shard_map/ppermute | solution.py:13
  922.4 7.8 all-to-all-start.27
  930.2 28.5 %all-to-all-done.27 = bf16[64,3,2048]{2,1,0:T(4,128)(2,1)} async-done(((bf16[64,3,2048]{2,1,0:T(4,128)(2,1)}), bf16[64,3,2048]{2,1,0:T(4,128)(2,1)}, u32[]{:S(2)}, u32[]{:S(2)}) %all-to-all-start.27) | async-done | bytes 786464 | tf_op jit(solution)/shard_map/all_to_all | solution.py:56
  958.6 9.7 conditional.24
  976.9 19.1 %all-to-all-done.28 = bf16[64,3,2048]{2,1,0:T(4,128)(2,1)} async-done(((bf16[64,3,2048]{2,1,0:T(4,128)(2,1)}), bf16[64,3,2048]{2,1,0:T(4,128)(2,1)}, u32[]{:S(2)}, u32[]{:S(2)}) %all-to-all-start.28) | async-done | bytes 786464 | tf_op jit(solution)/shard_map/all_to_all | solution.py:60
  1001.6 7.8 collective-permute-done.9
  1012.4 7.8 all-to-all-start.29
  1020.2 28.5 %all-to-all-done.29 = bf16[64,3,2048]{2,1,0:T(4,128)(2,1)} async-done(((bf16[64,3,2048]{2,1,0:T(4,128)(2,1)}), bf16[64,3,2048]{2,1,0:T(4,128)(2,1)}, u32[]{:S(2)}, u32[]{:S(2)}) %all-to-all-start.29) | async-done | bytes 786464 | tf_op jit(solution)/shard_map/all_to_all | solution.py:56
  1048.7 9.7 conditional.25
  1066.9 19.1 %all-to-all-done.30 = bf16[64,3,2048]{2,1,0:T(4,128)(2,1)} async-done(((bf16[64,3,2048]{2,1,0:T(4,128)(2,1)}), bf16[64,3,2048]{2,1,0:T(4,128)(2,1)}, u32[]{:S(2)}, u32[]{:S(2)}) %all-to-all-start.30) | async-done | bytes 786464 | tf_op jit(solution)/shard_map/all_to_all | solution.py:60
  1091.4 23.4 %collective-permute-done.10 = bf16[32,2048]{1,0:T(8,128)(2,1)S(1)} collective-permute-done((bf16[32,2048]{1,0:T(8,128)(2,1)S(1)}, bf16[32,2048]{1,0:T(8,128)(2,1)S(1)}, u32[]{:S(2)}, u32[]{:S(2)}) %collective-permute-start.10) | collective-permute-done | bytes 131104 | tf_op jit(solution)/shard_map/ppermute | solution.py:13
  1123.6 28.0 %all-to-all-done.31 = bf16[64,3,2048]{2,1,0:T(4,128)(2,1)} async-done(((bf16[64,3,2048]{2,1,0:T(4,128)(2,1)}), bf16[64,3,2048]{2,1,0:T(4,128)(2,1)}, u32[]{:S(2)}, u32[]{:S(2)}) %all-to-all-start.31) | async-done | bytes 786464 | tf_op jit(solution)/shard_map/all_to_all | solution.py:56
  1151.6 9.7 conditional.26
  1170.2 27.8 %all-to-all-done.32 = bf16[64,3,2048]{2,1,0:T(4,128)(2,1)} async-done(((bf16[64,3,2048]{2,1,0:T(4,128)(2,1)}), bf16[64,3,2048]{2,1,0:T(4,128)(2,1)}, u32[]{:S(2)}, u32[]{:S(2)}) %all-to-all-start.32) | async-done | bytes 786464 | tf_op jit(solution)/shard_map/all_to_all | solution.py:60
  1211.5 10.1 all-to-all-start.33
  1224.8 18.5 %all-to-all-done.33 = bf16[64,3,2048]{2,1,0:T(4,128)(2,1)} async-done(((bf16[64,3,2048]{2,1,0:T(4,128)(2,1)}), bf16[64,3,2048]{2,1,0:T(4,128)(2,1)}, u32[]{:S(2)}, u32[]{:S(2)}) %all-to-all-start.33) | async-done | bytes 786464 | tf_op jit(solution)/shard_map/all_to_all | solution.py:56
  1243.3 8.0 all-to-all-start.20
  1251.3 9.8 conditional.27
  1264.4 8.6 all-to-all-done.20
  1281.5 18.8 %all-to-all-done.34 = bf16[64,3,2048]{2,1,0:T(4,128)(2,1)S(1)} async-done(((bf16[64,3,2048]{2,1,0:T(4,128)(2,1)}), bf16[64,3,2048]{2,1,0:T(4,128)(2,1)S(1)}, u32[]{:S(2)}, u32[]{:S(2)}) %all-to-all-start.34) | async-done | bytes 786464 | tf_op jit(solution)/shard_map/all_to_all | solution.py:60
  1302.3 203.1 %psum.7 = f32[1,2048]{1,0:T(1,128)} all-reduce(f32[1,2048]{1,0:T(1,128)S(1)} %bitcast.633), channel_id=1, replica_groups=mesh['dp'=8,'pipe'=4,'expert'=8] {'dp','expert'}, use_global_device_ids=true, to_apply=%region_84.85 | all-reduce | flops 2048 | bytes 16384 | tf_op jit(solution)/shard_map/psum | solution.py:226
  (376 shorter events, 407.3 us)
Async XLA Ops:
  5.5 27.2 %all-to-all-start = ((bf16[64,3,1]{1,2,0:T(2,128)(2,1)}), bf16[64,3,1]{1,2,0:T(2,128)(2,1)S(1)}, u32[]{:S(2)}, u32[]{:S(2)}) async-start(bf16[64,3,1]{1,2,0:T(2,128)(2,1)} %copy.214), calls=%async_computation | async-start | bytes 65536 | tf_op jit(solution)/shard_map/all_to_all | solution.py:46
  32.7 33.2 %all-to-all-start.1 = ((bf16[64,3,2048]{2,1,0:T(4,128)(2,1)}), bf16[64,3,2048]{2,1,0:T(4,128)(2,1)}, u32[]{:S(2)}, u32[]{:S(2)}) async-start(bf16[64,3,2048]{2,1,0:T(4,128)(2,1)} %copy.215), calls=%async_computation.1 | async-start | bytes 2097152 | tf_op jit(solution)/shard_map/all_to_all | solution.py:45
  78.3 24.5 %all-to-all-start.2 = ((bf16[64,3,2048]{2,1,0:T(4,128)(2,1)}), bf16[64,3,2048]{2,1,0:T(4,128)(2,1)}, u32[]{:S(2)}, u32[]{:S(2)}) async-start(bf16[64,3,2048]{2,1,0:T(4,128)(2,1)} %reshape.639), calls=%async_computation.2 | async-start | bytes 2097152 | tf_op jit(solution)/shard_map/all_to_all | solution.py:52
  102.8 19.6 %all-to-all-start.3 = ((bf16[64,3,1]{1,2,0:T(2,128)(2,1)}), bf16[64,3,1]{1,2,0:T(2,128)(2,1)S(1)}, u32[]{:S(2)}, u32[]{:S(2)}) async-start(bf16[64,3,1]{1,2,0:T(2,128)(2,1)} %copy.218), calls=%async_computation.3 | async-start | bytes 65536 | tf_op jit(solution)/shard_map/all_to_all | solution.py:46
  107.5 10.6 copy-start.2
  107.6 12.7 copy-start.7
  109.9 10.4 copy-start.5
  109.9 9.6 collective-permute-start
  122.4 43.0 %all-to-all-start.4 = ((bf16[64,3,2048]{2,1,0:T(4,128)(2,1)}), bf16[64,3,2048]{2,1,0:T(4,128)(2,1)}, u32[]{:S(2)}, u32[]{:S(2)}) async-start(bf16[64,3,2048]{2,1,0:T(4,128)(2,1)} %copy.219), calls=%async_computation.4 | async-start | bytes 2097152 | tf_op jit(solution)/shard_map/all_to_all | solution.py:45
  178.0 24.5 %all-to-all-start.5 = ((bf16[64,3,2048]{2,1,0:T(4,128)(2,1)}), bf16[64,3,2048]{2,1,0:T(4,128)(2,1)}, u32[]{:S(2)}, u32[]{:S(2)}) async-start(bf16[64,3,2048]{2,1,0:T(4,128)(2,1)} %reshape.641), calls=%async_computation.5 | async-start | bytes 2097152 | tf_op jit(solution)/shard_map/all_to_all | solution.py:52
  205.4 23.7 %collective-permute-start.1 = (bf16[32,2048]{1,0:T(8,128)(2,1)S(1)}, bf16[32,2048]{1,0:T(8,128)(2,1)S(1)}, u32[]{:S(2)}, u32[]{:S(2)}) collective-permute-start(bf16[32,2048]{1,0:T(8,128)(2,1)S(1)} %get-tuple-element.841), channel_id=1, source_target_pairs={{0,8},{8,16},{16,24},{1,9},{9,17},{17,25},{2,10},{10,18},{18,26},{... | collective-permute-start | bytes 393224 | tf_op jit(solution)/shard_map/ppermute | solution.py:13
  224.3 16.5 %all-to-all-start.6 = ((bf16[64,3,1]{1,2,0:T(2,128)(2,1)}), bf16[64,3,1]{1,2,0:T(2,128)(2,1)S(1)}, u32[]{:S(2)}, u32[]{:S(2)}) async-start(bf16[64,3,1]{1,2,0:T(2,128)(2,1)} %copy.222), calls=%async_computation.6 | async-start | bytes 65536 | tf_op jit(solution)/shard_map/all_to_all | solution.py:46
  240.8 34.5 %all-to-all-start.7 = ((bf16[64,3,2048]{2,1,0:T(4,128)(2,1)}), bf16[64,3,2048]{2,1,0:T(4,128)(2,1)}, u32[]{:S(2)}, u32[]{:S(2)}) async-start(bf16[64,3,2048]{2,1,0:T(4,128)(2,1)} %copy.223), calls=%async_computation.7 | async-start | bytes 2097152 | tf_op jit(solution)/shard_map/all_to_all | solution.py:45
  284.4 12.5 copy-start.24
  287.7 31.1 %all-to-all-start.8 = ((bf16[64,3,2048]{2,1,0:T(4,128)(2,1)}), bf16[64,3,2048]{2,1,0:T(4,128)(2,1)}, u32[]{:S(2)}, u32[]{:S(2)}) async-start(bf16[64,3,2048]{2,1,0:T(4,128)(2,1)} %reshape.643), calls=%async_computation.8 | async-start | bytes 2097152 | tf_op jit(solution)/shard_map/all_to_all | solution.py:52
  321.7 11.8 collective-permute-start.2
  324.2 20.9 %all-to-all-start.9 = ((bf16[64,3,1]{1,2,0:T(2,128)(2,1)}), bf16[64,3,1]{1,2,0:T(2,128)(2,1)S(1)}, u32[]{:S(2)}, u32[]{:S(2)}) async-start(bf16[64,3,1]{1,2,0:T(2,128)(2,1)} %copy.226), calls=%async_computation.9 | async-start | bytes 65536 | tf_op jit(solution)/shard_map/all_to_all | solution.py:46
  345.1 32.7 %all-to-all-start.10 = ((bf16[64,3,2048]{2,1,0:T(4,128)(2,1)}), bf16[64,3,2048]{2,1,0:T(4,128)(2,1)}, u32[]{:S(2)}, u32[]{:S(2)}) async-start(bf16[64,3,2048]{2,1,0:T(4,128)(2,1)} %copy.227), calls=%async_computation.10 | async-start | bytes 2097152 | tf_op jit(solution)/shard_map/all_to_all | solution.py:45
  386.9 12.6 copy-start.23
  390.2 31.1 %all-to-all-start.11 = ((bf16[64,3,2048]{2,1,0:T(4,128)(2,1)}), bf16[64,3,2048]{2,1,0:T(4,128)(2,1)}, u32[]{:S(2)}, u32[]{:S(2)}) async-start(bf16[64,3,2048]{2,1,0:T(4,128)(2,1)} %reshape.645), calls=%async_computation.11 | async-start | bytes 2097152 | tf_op jit(solution)/shard_map/all_to_all | solution.py:52
  424.2 11.2 collective-permute-start.3
  426.2 20.7 %all-to-all-start.12 = ((bf16[64,3,1]{1,2,0:T(2,128)(2,1)}), bf16[64,3,1]{1,2,0:T(2,128)(2,1)S(1)}, u32[]{:S(2)}, u32[]{:S(2)}) async-start(bf16[64,3,1]{1,2,0:T(2,128)(2,1)} %copy.230), calls=%async_computation.12 | async-start | bytes 65536 | tf_op jit(solution)/shard_map/all_to_all | solution.py:46
  447.0 27.6 %all-to-all-start.13 = ((bf16[64,3,2048]{2,1,0:T(4,128)(2,1)}), bf16[64,3,2048]{2,1,0:T(4,128)(2,1)}, u32[]{:S(2)}, u32[]{:S(2)}) async-start(bf16[64,3,2048]{2,1,0:T(4,128)(2,1)} %copy.231), calls=%async_computation.13 | async-start | bytes 2097152 | tf_op jit(solution)/shard_map/all_to_all | solution.py:45
  476.6 8.9 copy-start.22
  479.9 30.7 %all-to-all-start.14 = ((bf16[64,3,2048]{2,1,0:T(4,128)(2,1)}), bf16[64,3,2048]{2,1,0:T(4,128)(2,1)}, u32[]{:S(2)}, u32[]{:S(2)}) async-start(bf16[64,3,2048]{2,1,0:T(4,128)(2,1)} %reshape.647), calls=%async_computation.14 | async-start | bytes 2097152 | tf_op jit(solution)/shard_map/all_to_all | solution.py:52
  513.5 11.1 collective-permute-start.4
  517.5 18.8 %all-to-all-start.15 = ((bf16[64,3,1]{1,2,0:T(2,128)(2,1)}), bf16[64,3,1]{1,2,0:T(2,128)(2,1)S(1)}, u32[]{:S(2)}, u32[]{:S(2)}) async-start(bf16[64,3,1]{1,2,0:T(2,128)(2,1)} %copy.234), calls=%async_computation.15 | async-start | bytes 65536 | tf_op jit(solution)/shard_map/all_to_all | solution.py:46
  536.3 28.2 %all-to-all-start.16 = ((bf16[64,3,2048]{2,1,0:T(4,128)(2,1)}), bf16[64,3,2048]{2,1,0:T(4,128)(2,1)}, u32[]{:S(2)}, u32[]{:S(2)}) async-start(bf16[64,3,2048]{2,1,0:T(4,128)(2,1)} %copy.235), calls=%async_computation.16 | async-start | bytes 2097152 | tf_op jit(solution)/shard_map/all_to_all | solution.py:45
  566.4 12.6 copy-start.21
  569.6 37.7 %all-to-all-start.17 = ((bf16[64,3,2048]{2,1,0:T(4,128)(2,1)}), bf16[64,3,2048]{2,1,0:T(4,128)(2,1)}, u32[]{:S(2)}, u32[]{:S(2)}) async-start(bf16[64,3,2048]{2,1,0:T(4,128)(2,1)} %reshape.649), calls=%async_computation.17 | async-start | bytes 2097152 | tf_op jit(solution)/shard_map/all_to_all | solution.py:52
  610.2 9.8 collective-permute-start.5
  612.5 19.1 %all-to-all-start.18 = ((bf16[64,3,1]{1,2,0:T(2,128)(2,1)}), bf16[64,3,1]{1,2,0:T(2,128)(2,1)S(1)}, u32[]{:S(2)}, u32[]{:S(2)}) async-start(bf16[64,3,1]{1,2,0:T(2,128)(2,1)} %copy.238), calls=%async_computation.18 | async-start | bytes 65536 | tf_op jit(solution)/shard_map/all_to_all | solution.py:46
  631.6 34.4 %all-to-all-start.19 = ((bf16[64,3,2048]{2,1,0:T(4,128)(2,1)}), bf16[64,3,2048]{2,1,0:T(4,128)(2,1)}, u32[]{:S(2)}, u32[]{:S(2)}) async-start(bf16[64,3,2048]{2,1,0:T(4,128)(2,1)} %copy.239), calls=%async_computation.19 | async-start | bytes 2097152 | tf_op jit(solution)/shard_map/all_to_all | solution.py:45
  666.0 24.4 %all-to-all-start.21 = ((bf16[64,3,2048]{2,1,0:T(4,128)(2,1)}), bf16[64,3,2048]{2,1,0:T(4,128)(2,1)}, u32[]{:S(2)}, u32[]{:S(2)}) async-start(bf16[64,3,2048]{2,1,0:T(4,128)(2,1)} %copy.242), calls=%async_computation.21 | async-start | bytes 2097152 | tf_op jit(solution)/shard_map/all_to_all | solution.py:56
  691.4 9.1 copy-start.20
  694.6 27.6 %copy-start.14 = (s32[64,32]{0,1:T(8,128)S(1)}, s32[64,32]{0,1:T(8,128)}, u32[]{:S(2)}) copy-start(s32[64,32]{0,1:T(8,128)} %copy-done.13) | copy-start | bytes 24580
  694.6 27.6 %all-to-all-start.22 = ((bf16[64,3,2048]{2,1,0:T(4,128)(2,1)}), bf16[64,3,2048]{2,1,0:T(4,128)(2,1)}, u32[]{:S(2)}, u32[]{:S(2)}) async-start(bf16[64,3,2048]{2,1,0:T(4,128)(2,1)} %reshape.654), calls=%async_computation.22 | async-start | bytes 2097152 | tf_op jit(solution)/shard_map/all_to_all | solution.py:60
  726.8 15.7 %collective-permute-start.6 = (bf16[32,2048]{1,0:T(8,128)(2,1)S(1)}, bf16[32,2048]{1,0:T(8,128)(2,1)S(1)}, u32[]{:S(2)}, u32[]{:S(2)}) collective-permute-start(bf16[32,2048]{1,0:T(8,128)(2,1)S(1)} %get-tuple-element.790), channel_id=1, source_target_pairs={{8,0},{16,8},{24,16},{9,1},{17,9},{25,17},{10,2},{18,10},{26,18},{... | collective-permute-start | bytes 393224 | tf_op jit(solution)/shard_map/ppermute | solution.py:13
  744.6 34.2 %all-to-all-start.23 = ((bf16[64,3,2048]{2,1,0:T(4,128)(2,1)}), bf16[64,3,2048]{2,1,0:T(4,128)(2,1)}, u32[]{:S(2)}, u32[]{:S(2)}) async-start(bf16[64,3,2048]{2,1,0:T(4,128)(2,1)} %copy.251), calls=%async_computation.23 | async-start | bytes 2097152 | tf_op jit(solution)/shard_map/all_to_all | solution.py:56
  783.1 24.3 %all-to-all-start.24 = ((bf16[64,3,2048]{2,1,0:T(4,128)(2,1)}), bf16[64,3,2048]{2,1,0:T(4,128)(2,1)}, u32[]{:S(2)}, u32[]{:S(2)}) async-start(bf16[64,3,2048]{2,1,0:T(4,128)(2,1)} %reshape.656), calls=%async_computation.24 | async-start | bytes 2097152 | tf_op jit(solution)/shard_map/all_to_all | solution.py:60
  811.5 12.8 collective-permute-start.7
  827.4 40.7 %all-to-all-start.25 = ((bf16[64,3,2048]{2,1,0:T(4,128)(2,1)}), bf16[64,3,2048]{2,1,0:T(4,128)(2,1)}, u32[]{:S(2)}, u32[]{:S(2)}) async-start(bf16[64,3,2048]{2,1,0:T(4,128)(2,1)} %copy.253), calls=%async_computation.25 | async-start | bytes 2097152 | tf_op jit(solution)/shard_map/all_to_all | solution.py:56
  869.2 8.4 copy-start.18
  872.5 24.3 %all-to-all-start.26 = ((bf16[64,3,2048]{2,1,0:T(4,128)(2,1)}), bf16[64,3,2048]{2,1,0:T(4,128)(2,1)}, u32[]{:S(2)}, u32[]{:S(2)}) async-start(bf16[64,3,2048]{2,1,0:T(4,128)(2,1)} %reshape.658), calls=%async_computation.26 | async-start | bytes 2097152 | tf_op jit(solution)/shard_map/all_to_all | solution.py:60
  900.9 18.4 %collective-permute-start.8 = (bf16[32,2048]{1,0:T(8,128)(2,1)S(1)}, bf16[32,2048]{1,0:T(8,128)(2,1)S(1)}, u32[]{:S(2)}, u32[]{:S(2)}) collective-permute-start(bf16[32,2048]{1,0:T(8,128)(2,1)S(1)} %get-tuple-element.786), channel_id=1, source_target_pairs={{8,0},{16,8},{24,16},{9,1},{17,9},{25,17},{10,2},{18,10},{26,18},{... | collective-permute-start | bytes 393224 | tf_op jit(solution)/shard_map/ppermute | solution.py:13
  922.4 36.3 %all-to-all-start.27 = ((bf16[64,3,2048]{2,1,0:T(4,128)(2,1)}), bf16[64,3,2048]{2,1,0:T(4,128)(2,1)}, u32[]{:S(2)}, u32[]{:S(2)}) async-start(bf16[64,3,2048]{2,1,0:T(4,128)(2,1)} %copy.255), calls=%async_computation.27 | async-start | bytes 2097152 | tf_op jit(solution)/shard_map/all_to_all | solution.py:56
  968.3 8.4 copy-start.17
  971.6 24.4 %all-to-all-start.28 = ((bf16[64,3,2048]{2,1,0:T(4,128)(2,1)}), bf16[64,3,2048]{2,1,0:T(4,128)(2,1)}, u32[]{:S(2)}, u32[]{:S(2)}) async-start(bf16[64,3,2048]{2,1,0:T(4,128)(2,1)} %reshape.660), calls=%async_computation.28 | async-start | bytes 2097152 | tf_op jit(solution)/shard_map/all_to_all | solution.py:60
  1000.1 9.3 collective-permute-start.9
  1012.4 36.3 %all-to-all-start.29 = ((bf16[64,3,2048]{2,1,0:T(4,128)(2,1)}), bf16[64,3,2048]{2,1,0:T(4,128)(2,1)}, u32[]{:S(2)}, u32[]{:S(2)}) async-start(bf16[64,3,2048]{2,1,0:T(4,128)(2,1)} %copy.257), calls=%async_computation.29 | async-start | bytes 2097152 | tf_op jit(solution)/shard_map/all_to_all | solution.py:56
  1058.4 8.4 copy-start.16
  1058.4 8.5 copy-start.27
  1061.6 24.4 %all-to-all-start.30 = ((bf16[64,3,2048]{2,1,0:T(4,128)(2,1)}), bf16[64,3,2048]{2,1,0:T(4,128)(2,1)}, u32[]{:S(2)}, u32[]{:S(2)}) async-start(bf16[64,3,2048]{2,1,0:T(4,128)(2,1)} %reshape.662), calls=%async_computation.30 | async-start | bytes 2097152 | tf_op jit(solution)/shard_map/all_to_all | solution.py:60
  1090.1 24.7 %collective-permute-start.10 = (bf16[32,2048]{1,0:T(8,128)(2,1)S(1)}, bf16[32,2048]{1,0:T(8,128)(2,1)S(1)}, u32[]{:S(2)}, u32[]{:S(2)}) collective-permute-start(bf16[32,2048]{1,0:T(8,128)(2,1)S(1)} %get-tuple-element.782), channel_id=1, source_target_pairs={{8,0},{16,8},{24,16},{9,1},{17,9},{25,17},{10,2},{18,10},{26,18},{... | collective-permute-start | bytes 393224 | tf_op jit(solution)/shard_map/ppermute | solution.py:13
  1117.9 33.7 %all-to-all-start.31 = ((bf16[64,3,2048]{2,1,0:T(4,128)(2,1)}), bf16[64,3,2048]{2,1,0:T(4,128)(2,1)}, u32[]{:S(2)}, u32[]{:S(2)}) async-start(bf16[64,3,2048]{2,1,0:T(4,128)(2,1)} %copy.259), calls=%async_computation.31 | async-start | bytes 2097152 | tf_op jit(solution)/shard_map/all_to_all | solution.py:56
  1161.3 8.8 copy-start.15
  1161.3 8.9 copy-start.26
  1164.6 33.5 %all-to-all-start.32 = ((bf16[64,3,2048]{2,1,0:T(4,128)(2,1)}), bf16[64,3,2048]{2,1,0:T(4,128)(2,1)}, u32[]{:S(2)}, u32[]{:S(2)}) async-start(bf16[64,3,2048]{2,1,0:T(4,128)(2,1)} %reshape.664), calls=%async_computation.32 | async-start | bytes 2097152 | tf_op jit(solution)/shard_map/all_to_all | solution.py:60
  1202.1 6.4 collective-permute-start.11
  1211.5 31.9 %all-to-all-start.33 = ((bf16[64,3,2048]{2,1,0:T(4,128)(2,1)}), bf16[64,3,2048]{2,1,0:T(4,128)(2,1)}, u32[]{:S(2)}, u32[]{:S(2)}) async-start(bf16[64,3,2048]{2,1,0:T(4,128)(2,1)} %copy.261), calls=%async_computation.33 | async-start | bytes 2097152 | tf_op jit(solution)/shard_map/all_to_all | solution.py:56
  1243.3 29.7 %all-to-all-start.20 = ((bf16[64,3,2048]{2,1,0:T(4,128)(2,1)}), bf16[64,3,2048]{2,1,0:T(4,128)(2,1)}, u32[]{:S(2)}, u32[]{:S(2)}) async-start(bf16[64,3,2048]{2,1,0:T(4,128)(2,1)} %reshape.651), calls=%async_computation.20 | async-start | bytes 2097152 | tf_op jit(solution)/shard_map/all_to_all | solution.py:52
  1261.1 17.2 %copy-start.6 = (bf16[5,32,2048]{2,1,0:T(8,128)(2,1)S(1)}, bf16[5,32,2048]{2,1,0:T(8,128)(2,1)}, u32[]{:S(2)}) copy-start(bf16[5,32,2048]{2,1,0:T(8,128)(2,1)} %get-tuple-element.848) | copy-start | bytes 1966084
  1273.1 27.2 %all-to-all-start.34 = ((bf16[64,3,2048]{2,1,0:T(4,128)(2,1)}), bf16[64,3,2048]{2,1,0:T(4,128)(2,1)S(1)}, u32[]{:S(2)}, u32[]{:S(2)}) async-start(bf16[64,3,2048]{2,1,0:T(4,128)(2,1)} %reshape.666), calls=%async_computation.34 | async-start | bytes 2097152 | tf_op jit(solution)/shard_map/all_to_all | solution.py:60
  1278.3 227.0 %copy-start.4 = (bf16[5,32,2048]{2,1,0:T(8,128)(2,1)S(1)}, bf16[5,32,2048]{2,1,0:T(8,128)(2,1)}, u32[]{:S(2)}) copy-start(bf16[5,32,2048]{2,1,0:T(8,128)(2,1)} %get-tuple-element.779) | copy-start | bytes 1966084
  (11 other events, 21.7 us)
where the time goes:
time: 1520 us; the launch traced here: 1510 us
  waiting for transfers between devices  747 us (49%)
  starting transfers between devices  290 us (19%)
  blocking collectives  203 us (13%)
  local copies, waits for them, and re-layouts  141 us (9%)
  matrix products  92.5 us (6%)
  other arithmetic  31.6 us (2%)
    psum x1, blocking collectives, body(): gain_grad = lax.psum(gain_sum, ('dp', 'expert'))  203 us
    all_to_all x7, waiting for transfers between devices, send_rows(): lax.all_to_all(row_block, ('dp', 'expert'), split_axis=0, concat_axis=0,...  177 us
    all_to_all x7, waiting for transfers between devices, send_grads(): lax.all_to_all(row_block, ('dp', 'expert'), split_axis=0, concat_axis=0,...  165 us
    all_to_all x7, waiting for transfers between devices, return_grads(): lax.all_to_all(row_block, ('dp', 'expert'), split_axis=0, concat_axis=0,...  144 us
    all_to_all x7, waiting for transfers between devices, return_rows(): lax.all_to_all(row_block, ('dp', 'expert'), split_axis=0, concat_axis=0,...  138 us
    ppermute x12, waiting for transfers between devices, from_behind(): lax.ppermute(value, axis, [(source, source + steps) for source in range(l...  79.9 us
    all_to_all x7, starting transfers between devices, send_rows(): lax.all_to_all(pair_block, ('dp', 'expert'), split_axis=0, concat_axis=0,...  58 us
    all_to_all x7, starting transfers between devices, send_grads(): lax.all_to_all(row_block, ('dp', 'expert'), split_axis=0, concat_axis=0,...  54.3 us
  transfers between devices with their start and end apart: 47, of which 41 were waited for; matrix products, arithmetic and copies ran while one was open for 5% of the time, Pallas kernels for 0%

commit v1 on v0

--- a/solution.py
+++ b/solution.py
@@ -2,6 +2,7 @@
 import jax.numpy as jnp
 from jax import lax
 from jax.sharding import PartitionSpec as P
+from jax.lax import all_gather
 
 MICRO = 4
 epsilon = 1e-06
@@ -223,7 +224,7 @@
         gain_sum = gain_sum + gain_term
         if tick_num + 1 < ticks:
             incoming = from_behind(grad_bf, "pipe", -1)
-    gain_grad = lax.psum(gain_sum, ("dp", "expert"))
+    gain_grad = jnp.sum(all_gather(gain_sum, ("dp", "expert")), 0)
     segment_out = layer_outs[:MICRO].reshape(1, tok_rows, width)
     segment_grad = grad_outs[:MICRO].reshape(1, tok_rows, width)
     return (segment_out, segment_grad, gain_grad.reshape(1, width))

time: 1520 us -> 1430 us (0.941)
  blocking collectives: 203 us -> 111 us
    psum x1 -> x0, blocking collectives: 203 us -> none  [body(): gain_grad = lax.psum(gain_sum, ('dp', 'expert'))]
    all_gather x0 -> x1, blocking collectives: none -> 111 us  [body(): gain_grad = jnp.sum(all_gather(gain_sum, ('dp', 'expert')), 0)]
  transfers between devices with their start and end apart: 47 -> 47, of which waited for: 41 -> 41; matrix products, arithmetic and copies ran while one was open for 5% -> 6% of each run, Pallas kernels for 0% -> 0%
where the time goes in v1:
time: 1430 us; the launch traced here: 1420 us
  waiting for transfers between devices  747 us (52%)
  starting transfers between devices  290 us (20%)
  local copies, waits for them, and re-layouts  141 us (10%)
  blocking collectives  111 us (8%)
  matrix products  92.5 us (6%)
  other arithmetic  32.3 us (2%)
    all_to_all x7, waiting for transfers between devices, send_rows(): lax.all_to_all(row_block, ('dp', 'expert'), split_axis=0, concat_axis=0,...  177 us
    all_to_all x7, waiting for transfers between devices, send_grads(): lax.all_to_all(row_block, ('dp', 'expert'), split_axis=0, concat_axis=0,...  165 us
    all_to_all x7, waiting for transfers between devices, return_grads(): lax.all_to_all(row_block, ('dp', 'expert'), split_axis=0, concat_axis=0,...  144 us
    all_to_all x7, waiting for transfers between devices, return_rows(): lax.all_to_all(row_block, ('dp', 'expert'), split_axis=0, concat_axis=0,...  138 us
    all_gather x1, blocking collectives, body(): gain_grad = jnp.sum(all_gather(gain_sum, ('dp', 'expert')), 0)  111 us
    ppermute x12, waiting for transfers between devices, from_behind(): lax.ppermute(value, axis, [(source, source + steps) for source in range(l...  79.9 us
    all_to_all x7, starting transfers between devices, send_rows(): lax.all_to_all(pair_block, ('dp', 'expert'), split_axis=0, concat_axis=0,...  58 us
    all_to_all x7, starting transfers between devices, send_grads(): lax.all_to_all(row_block, ('dp', 'expert'), split_axis=0, concat_axis=0,...  54.3 us
  transfers between devices with their start and end apart: 47, of which 41 were waited for; matrix products, arithmetic and copies ran while one was open for 6% of the time, Pallas kernels for 0%

profile of v1, /device:TPU:1, one launch (start us, length us, event | category | flops | bytes accessed | tf_op | source)
XLA Modules:
  0.0 1416.8 jit_solution(5256557095046495706)
XLA Ops:
  5.5 15.6 %all-to-all-start = ((bf16[64,3,1]{1,2,0:T(2,128)(2,1)}), bf16[64,3,1]{1,2,0:T(2,128)(2,1)S(1)}, u32[]{:S(2)}, u32[]{:S(2)}) async-start(bf16[64,3,1]{1,2,0:T(2,128)(2,1)} %copy.214), calls=%async_computation | async-start | bytes 65536 | tf_op jit(solution)/shard_map/all_to_all | solution.py:47
  25.2 7.5 all-to-all-done
  40.4 25.5 %all-to-all-done.1 = bf16[64,3,2048]{2,1,0:T(4,128)(2,1)} async-done(((bf16[64,3,2048]{2,1,0:T(4,128)(2,1)}), bf16[64,3,2048]{2,1,0:T(4,128)(2,1)}, u32[]{:S(2)}, u32[]{:S(2)}) %all-to-all-start.1) | async-done | bytes 786464 | tf_op jit(solution)/shard_map/all_to_all | solution.py:46
  65.9 9.1 conditional.14
  84.8 18.1 %all-to-all-done.2 = bf16[64,3,2048]{2,1,0:T(4,128)(2,1)} async-done(((bf16[64,3,2048]{2,1,0:T(4,128)(2,1)}), bf16[64,3,2048]{2,1,0:T(4,128)(2,1)}, u32[]{:S(2)}, u32[]{:S(2)}) %all-to-all-start.2) | async-done | bytes 786464 | tf_op jit(solution)/shard_map/all_to_all | solution.py:53
  109.9 7.3 collective-permute-start
  122.4 14.5 %all-to-all-start.4 = ((bf16[64,3,2048]{2,1,0:T(4,128)(2,1)}), bf16[64,3,2048]{2,1,0:T(4,128)(2,1)}, u32[]{:S(2)}, u32[]{:S(2)}) async-start(bf16[64,3,2048]{2,1,0:T(4,128)(2,1)} %copy.219), calls=%async_computation.4 | async-start | bytes 2097152 | tf_op jit(solution)/shard_map/all_to_all | solution.py:46
  136.9 28.5 %all-to-all-done.4 = bf16[64,3,2048]{2,1,0:T(4,128)(2,1)} async-done(((bf16[64,3,2048]{2,1,0:T(4,128)(2,1)}), bf16[64,3,2048]{2,1,0:T(4,128)(2,1)}, u32[]{:S(2)}, u32[]{:S(2)}) %all-to-all-start.4) | async-done | bytes 786464 | tf_op jit(solution)/shard_map/all_to_all | solution.py:46
  165.4 9.3 conditional.15
  184.1 18.4 %all-to-all-done.5 = bf16[64,3,2048]{2,1,0:T(4,128)(2,1)} async-done(((bf16[64,3,2048]{2,1,0:T(4,128)(2,1)}), bf16[64,3,2048]{2,1,0:T(4,128)(2,1)}, u32[]{:S(2)}, u32[]{:S(2)}) %all-to-all-start.5) | async-done | bytes 786464 | tf_op jit(solution)/shard_map/all_to_all | solution.py:53
  205.4 17.4 %collective-permute-start.1 = (bf16[32,2048]{1,0:T(8,128)(2,1)S(1)}, bf16[32,2048]{1,0:T(8,128)(2,1)S(1)}, u32[]{:S(2)}, u32[]{:S(2)}) collective-permute-start(bf16[32,2048]{1,0:T(8,128)(2,1)S(1)} %get-tuple-element.841), channel_id=1, source_target_pairs={{0,8},{8,16},{16,24},{1,9},{9,17},{17,25},{2,10},{10,18},{18,26},{... | collective-permute-start | bytes 393224 | tf_op jit(solution)/shard_map/ppermute | solution.py:14
  233.7 7.2 all-to-all-done.6
  240.8 5.9 all-to-all-start.7
  246.7 28.6 %all-to-all-done.7 = bf16[64,3,2048]{2,1,0:T(4,128)(2,1)} async-done(((bf16[64,3,2048]{2,1,0:T(4,128)(2,1)}), bf16[64,3,2048]{2,1,0:T(4,128)(2,1)}, u32[]{:S(2)}, u32[]{:S(2)}) %all-to-all-start.7) | async-done | bytes 786464 | tf_op jit(solution)/shard_map/all_to_all | solution.py:46
  275.3 9.1 conditional.16
  287.7 9.0 all-to-all-start.8
  298.6 20.2 %all-to-all-done.8 = bf16[64,3,2048]{2,1,0:T(4,128)(2,1)} async-done(((bf16[64,3,2048]{2,1,0:T(4,128)(2,1)}), bf16[64,3,2048]{2,1,0:T(4,128)(2,1)}, u32[]{:S(2)}, u32[]{:S(2)}) %all-to-all-start.8) | async-done | bytes 786464 | tf_op jit(solution)/shard_map/all_to_all | solution.py:53
  324.2 9.3 all-to-all-start.9
  338.0 7.1 all-to-all-done.9
  350.9 26.9 %all-to-all-done.10 = bf16[64,3,2048]{2,1,0:T(4,128)(2,1)} async-done(((bf16[64,3,2048]{2,1,0:T(4,128)(2,1)}), bf16[64,3,2048]{2,1,0:T(4,128)(2,1)}, u32[]{:S(2)}, u32[]{:S(2)}) %all-to-all-start.10) | async-done | bytes 786464 | tf_op jit(solution)/shard_map/all_to_all | solution.py:46
  377.8 9.1 conditional.17
  390.2 9.2 all-to-all-start.11
  399.7 21.5 %all-to-all-done.11 = bf16[64,3,2048]{2,1,0:T(4,128)(2,1)} async-done(((bf16[64,3,2048]{2,1,0:T(4,128)(2,1)}), bf16[64,3,2048]{2,1,0:T(4,128)(2,1)}, u32[]{:S(2)}, u32[]{:S(2)}) %all-to-all-start.11) | async-done | bytes 786464 | tf_op jit(solution)/shard_map/all_to_all | solution.py:53
  426.2 9.1 all-to-all-start.12
  439.9 7.1 all-to-all-done.12
  452.8 21.8 %all-to-all-done.13 = bf16[64,3,2048]{2,1,0:T(4,128)(2,1)} async-done(((bf16[64,3,2048]{2,1,0:T(4,128)(2,1)}), bf16[64,3,2048]{2,1,0:T(4,128)(2,1)}, u32[]{:S(2)}, u32[]{:S(2)}) %all-to-all-start.13) | async-done | bytes 786464 | tf_op jit(solution)/shard_map/all_to_all | solution.py:46
  486.5 24.1 %all-to-all-done.14 = bf16[64,3,2048]{2,1,0:T(4,128)(2,1)} async-done(((bf16[64,3,2048]{2,1,0:T(4,128)(2,1)}), bf16[64,3,2048]{2,1,0:T(4,128)(2,1)}, u32[]{:S(2)}, u32[]{:S(2)}) %all-to-all-start.14) | async-done | bytes 786464 | tf_op jit(solution)/shard_map/all_to_all | solution.py:53
  517.5 7.1 all-to-all-start.15
  529.1 7.2 all-to-all-done.15
  542.1 22.4 %all-to-all-done.16 = bf16[64,3,2048]{2,1,0:T(4,128)(2,1)} async-done(((bf16[64,3,2048]{2,1,0:T(4,128)(2,1)}), bf16[64,3,2048]{2,1,0:T(4,128)(2,1)}, u32[]{:S(2)}, u32[]{:S(2)}) %all-to-all-start.16) | async-done | bytes 786464 | tf_op jit(solution)/shard_map/all_to_all | solution.py:46
  569.6 9.2 all-to-all-start.17
  580.6 26.7 %all-to-all-done.17 = bf16[64,3,2048]{2,1,0:T(4,128)(2,1)} async-done(((bf16[64,3,2048]{2,1,0:T(4,128)(2,1)}), bf16[64,3,2048]{2,1,0:T(4,128)(2,1)}, u32[]{:S(2)}, u32[]{:S(2)}) %all-to-all-start.17) | async-done | bytes 786464 | tf_op jit(solution)/shard_map/all_to_all | solution.py:53
  612.5 7.5 all-to-all-start.18
  624.5 7.1 all-to-all-done.18
  642.5 23.4 %all-to-all-done.19 = bf16[64,3,2048]{2,1,0:T(4,128)(2,1)} async-done(((bf16[64,3,2048]{2,1,0:T(4,128)(2,1)}), bf16[64,3,2048]{2,1,0:T(4,128)(2,1)}, u32[]{:S(2)}, u32[]{:S(2)}) %all-to-all-start.19) | async-done | bytes 786464 | tf_op jit(solution)/shard_map/all_to_all | solution.py:46
  701.7 20.6 %all-to-all-done.22 = bf16[64,3,2048]{2,1,0:T(4,128)(2,1)} async-done(((bf16[64,3,2048]{2,1,0:T(4,128)(2,1)}), bf16[64,3,2048]{2,1,0:T(4,128)(2,1)}, u32[]{:S(2)}, u32[]{:S(2)}) %all-to-all-start.22) | async-done | bytes 786464 | tf_op jit(solution)/shard_map/all_to_all | solution.py:61
  728.1 14.4 %collective-permute-done.6 = bf16[32,2048]{1,0:T(8,128)(2,1)S(1)} collective-permute-done((bf16[32,2048]{1,0:T(8,128)(2,1)S(1)}, bf16[32,2048]{1,0:T(8,128)(2,1)S(1)}, u32[]{:S(2)}, u32[]{:S(2)}) %collective-permute-start.6) | collective-permute-done | bytes 131104 | tf_op jit(solution)/shard_map/ppermute | solution.py:14
  750.4 28.5 %all-to-all-done.23 = bf16[64,3,2048]{2,1,0:T(4,128)(2,1)} async-done(((bf16[64,3,2048]{2,1,0:T(4,128)(2,1)}), bf16[64,3,2048]{2,1,0:T(4,128)(2,1)}, u32[]{:S(2)}, u32[]{:S(2)}) %all-to-all-start.23) | async-done | bytes 786464 | tf_op jit(solution)/shard_map/all_to_all | solution.py:57
  788.4 19.0 %all-to-all-done.24 = bf16[64,3,2048]{2,1,0:T(4,128)(2,1)} async-done(((bf16[64,3,2048]{2,1,0:T(4,128)(2,1)}), bf16[64,3,2048]{2,1,0:T(4,128)(2,1)}, u32[]{:S(2)}, u32[]{:S(2)}) %all-to-all-start.24) | async-done | bytes 786464 | tf_op jit(solution)/shard_map/all_to_all | solution.py:61
  812.8 11.5 collective-permute-done.7
  827.4 12.2 all-to-all-start.25
  839.6 28.5 %all-to-all-done.25 = bf16[64,3,2048]{2,1,0:T(4,128)(2,1)} async-done(((bf16[64,3,2048]{2,1,0:T(4,128)(2,1)}), bf16[64,3,2048]{2,1,0:T(4,128)(2,1)}, u32[]{:S(2)}, u32[]{:S(2)}) %all-to-all-start.25) | async-done | bytes 786464 | tf_op jit(solution)/shard_map/all_to_all | solution.py:57
  877.8 19.0 %all-to-all-done.26 = bf16[64,3,2048]{2,1,0:T(4,128)(2,1)} async-done(((bf16[64,3,2048]{2,1,0:T(4,128)(2,1)}), bf16[64,3,2048]{2,1,0:T(4,128)(2,1)}, u32[]{:S(2)}, u32[]{:S(2)}) %all-to-all-start.26) | async-done | bytes 786464 | tf_op jit(solution)/shard_map/all_to_all | solution.py:61
  902.2 17.1 %collective-permute-done.8 = bf16[32,2048]{1,0:T(8,128)(2,1)S(1)} collective-permute-done((bf16[32,2048]{1,0:T(8,128)(2,1)S(1)}, bf16[32,2048]{1,0:T(8,128)(2,1)S(1)}, u32[]{:S(2)}, u32[]{:S(2)}) %collective-permute-start.8) | collective-permute-done | bytes 131104 | tf_op jit(solution)/shard_map/ppermute | solution.py:14
  922.4 7.8 all-to-all-start.27
  930.2 28.5 %all-to-all-done.27 = bf16[64,3,2048]{2,1,0:T(4,128)(2,1)} async-done(((bf16[64,3,2048]{2,1,0:T(4,128)(2,1)}), bf16[64,3,2048]{2,1,0:T(4,128)(2,1)}, u32[]{:S(2)}, u32[]{:S(2)}) %all-to-all-start.27) | async-done | bytes 786464 | tf_op jit(solution)/shard_map/all_to_all | solution.py:57
  958.6 9.7 conditional.24
  976.9 19.1 %all-to-all-done.28 = bf16[64,3,2048]{2,1,0:T(4,128)(2,1)} async-done(((bf16[64,3,2048]{2,1,0:T(4,128)(2,1)}), bf16[64,3,2048]{2,1,0:T(4,128)(2,1)}, u32[]{:S(2)}, u32[]{:S(2)}) %all-to-all-start.28) | async-done | bytes 786464 | tf_op jit(solution)/shard_map/all_to_all | solution.py:61
  1001.6 7.8 collective-permute-done.9
  1012.4 7.8 all-to-all-start.29
  1020.2 28.5 %all-to-all-done.29 = bf16[64,3,2048]{2,1,0:T(4,128)(2,1)} async-done(((bf16[64,3,2048]{2,1,0:T(4,128)(2,1)}), bf16[64,3,2048]{2,1,0:T(4,128)(2,1)}, u32[]{:S(2)}, u32[]{:S(2)}) %all-to-all-start.29) | async-done | bytes 786464 | tf_op jit(solution)/shard_map/all_to_all | solution.py:57
  1048.7 9.7 conditional.25
  1066.9 19.1 %all-to-all-done.30 = bf16[64,3,2048]{2,1,0:T(4,128)(2,1)} async-done(((bf16[64,3,2048]{2,1,0:T(4,128)(2,1)}), bf16[64,3,2048]{2,1,0:T(4,128)(2,1)}, u32[]{:S(2)}, u32[]{:S(2)}) %all-to-all-start.30) | async-done | bytes 786464 | tf_op jit(solution)/shard_map/all_to_all | solution.py:61
  1091.4 23.4 %collective-permute-done.10 = bf16[32,2048]{1,0:T(8,128)(2,1)S(1)} collective-permute-done((bf16[32,2048]{1,0:T(8,128)(2,1)S(1)}, bf16[32,2048]{1,0:T(8,128)(2,1)S(1)}, u32[]{:S(2)}, u32[]{:S(2)}) %collective-permute-start.10) | collective-permute-done | bytes 131104 | tf_op jit(solution)/shard_map/ppermute | solution.py:14
  1123.6 28.0 %all-to-all-done.31 = bf16[64,3,2048]{2,1,0:T(4,128)(2,1)} async-done(((bf16[64,3,2048]{2,1,0:T(4,128)(2,1)}), bf16[64,3,2048]{2,1,0:T(4,128)(2,1)}, u32[]{:S(2)}, u32[]{:S(2)}) %all-to-all-start.31) | async-done | bytes 786464 | tf_op jit(solution)/shard_map/all_to_all | solution.py:57
  1151.6 9.7 conditional.26
  1170.2 27.8 %all-to-all-done.32 = bf16[64,3,2048]{2,1,0:T(4,128)(2,1)} async-done(((bf16[64,3,2048]{2,1,0:T(4,128)(2,1)}), bf16[64,3,2048]{2,1,0:T(4,128)(2,1)}, u32[]{:S(2)}, u32[]{:S(2)}) %all-to-all-start.32) | async-done | bytes 786464 | tf_op jit(solution)/shard_map/all_to_all | solution.py:61
  1211.5 10.1 all-to-all-start.33
  1224.8 18.5 %all-to-all-done.33 = bf16[64,3,2048]{2,1,0:T(4,128)(2,1)} async-done(((bf16[64,3,2048]{2,1,0:T(4,128)(2,1)}), bf16[64,3,2048]{2,1,0:T(4,128)(2,1)}, u32[]{:S(2)}, u32[]{:S(2)}) %all-to-all-start.33) | async-done | bytes 786464 | tf_op jit(solution)/shard_map/all_to_all | solution.py:57
  1243.3 8.0 all-to-all-start.20
  1251.3 9.8 conditional.27
  1264.4 8.6 all-to-all-done.20
  1281.4 19.0 %all-to-all-done.34 = bf16[64,3,2048]{2,1,0:T(4,128)(2,1)S(1)} async-done(((bf16[64,3,2048]{2,1,0:T(4,128)(2,1)}), bf16[64,3,2048]{2,1,0:T(4,128)(2,1)S(1)}, u32[]{:S(2)}, u32[]{:S(2)}) %all-to-all-start.34) | async-done | bytes 786464 | tf_op jit(solution)/shard_map/all_to_all | solution.py:61
  1302.3 111.4 %all-gather = f32[131072]{0:T(1024)S(1)} all-gather(f32[2048]{0:T(1024)S(1)} %add_add_fusion), channel_id=2, replica_groups=mesh['dp'=8,'pipe'=4,'expert'=8] {'dp','expert'}, dimensions={0}, use_global_device_ids=true | all-gather | bytes 532480 | tf_op jit(solution)/shard_map/all_gather | solution.py:227
  (378 shorter events, 407.9 us)
Async XLA Ops:
  5.5 27.2 %all-to-all-start = ((bf16[64,3,1]{1,2,0:T(2,128)(2,1)}), bf16[64,3,1]{1,2,0:T(2,128)(2,1)S(1)}, u32[]{:S(2)}, u32[]{:S(2)}) async-start(bf16[64,3,1]{1,2,0:T(2,128)(2,1)} %copy.214), calls=%async_computation | async-start | bytes 65536 | tf_op jit(solution)/shard_map/all_to_all | solution.py:47
  32.7 33.2 %all-to-all-start.1 = ((bf16[64,3,2048]{2,1,0:T(4,128)(2,1)}), bf16[64,3,2048]{2,1,0:T(4,128)(2,1)}, u32[]{:S(2)}, u32[]{:S(2)}) async-start(bf16[64,3,2048]{2,1,0:T(4,128)(2,1)} %copy.215), calls=%async_computation.1 | async-start | bytes 2097152 | tf_op jit(solution)/shard_map/all_to_all | solution.py:46
  78.3 24.5 %all-to-all-start.2 = ((bf16[64,3,2048]{2,1,0:T(4,128)(2,1)}), bf16[64,3,2048]{2,1,0:T(4,128)(2,1)}, u32[]{:S(2)}, u32[]{:S(2)}) async-start(bf16[64,3,2048]{2,1,0:T(4,128)(2,1)} %reshape.730), calls=%async_computation.2 | async-start | bytes 2097152 | tf_op jit(solution)/shard_map/all_to_all | solution.py:53
  102.8 19.6 %all-to-all-start.3 = ((bf16[64,3,1]{1,2,0:T(2,128)(2,1)}), bf16[64,3,1]{1,2,0:T(2,128)(2,1)S(1)}, u32[]{:S(2)}, u32[]{:S(2)}) async-start(bf16[64,3,1]{1,2,0:T(2,128)(2,1)} %copy.218), calls=%async_computation.3 | async-start | bytes 65536 | tf_op jit(solution)/shard_map/all_to_all | solution.py:47
  107.5 10.6 copy-start.2
  107.6 12.7 copy-start.7
  109.9 10.4 copy-start.5
  109.9 9.6 collective-permute-start
  122.4 43.0 %all-to-all-start.4 = ((bf16[64,3,2048]{2,1,0:T(4,128)(2,1)}), bf16[64,3,2048]{2,1,0:T(4,128)(2,1)}, u32[]{:S(2)}, u32[]{:S(2)}) async-start(bf16[64,3,2048]{2,1,0:T(4,128)(2,1)} %copy.219), calls=%async_computation.4 | async-start | bytes 2097152 | tf_op jit(solution)/shard_map/all_to_all | solution.py:46
  178.0 24.5 %all-to-all-start.5 = ((bf16[64,3,2048]{2,1,0:T(4,128)(2,1)}), bf16[64,3,2048]{2,1,0:T(4,128)(2,1)}, u32[]{:S(2)}, u32[]{:S(2)}) async-start(bf16[64,3,2048]{2,1,0:T(4,128)(2,1)} %reshape.732), calls=%async_computation.5 | async-start | bytes 2097152 | tf_op jit(solution)/shard_map/all_to_all | solution.py:53
  205.4 23.7 %collective-permute-start.1 = (bf16[32,2048]{1,0:T(8,128)(2,1)S(1)}, bf16[32,2048]{1,0:T(8,128)(2,1)S(1)}, u32[]{:S(2)}, u32[]{:S(2)}) collective-permute-start(bf16[32,2048]{1,0:T(8,128)(2,1)S(1)} %get-tuple-element.841), channel_id=1, source_target_pairs={{0,8},{8,16},{16,24},{1,9},{9,17},{17,25},{2,10},{10,18},{18,26},{... | collective-permute-start | bytes 393224 | tf_op jit(solution)/shard_map/ppermute | solution.py:14
  224.3 16.5 %all-to-all-start.6 = ((bf16[64,3,1]{1,2,0:T(2,128)(2,1)}), bf16[64,3,1]{1,2,0:T(2,128)(2,1)S(1)}, u32[]{:S(2)}, u32[]{:S(2)}) async-start(bf16[64,3,1]{1,2,0:T(2,128)(2,1)} %copy.222), calls=%async_computation.6 | async-start | bytes 65536 | tf_op jit(solution)/shard_map/all_to_all | solution.py:47
  240.8 34.5 %all-to-all-start.7 = ((bf16[64,3,2048]{2,1,0:T(4,128)(2,1)}), bf16[64,3,2048]{2,1,0:T(4,128)(2,1)}, u32[]{:S(2)}, u32[]{:S(2)}) async-start(bf16[64,3,2048]{2,1,0:T(4,128)(2,1)} %copy.223), calls=%async_computation.7 | async-start | bytes 2097152 | tf_op jit(solution)/shard_map/all_to_all | solution.py:46
  284.4 12.5 copy-start.24
  287.7 31.1 %all-to-all-start.8 = ((bf16[64,3,2048]{2,1,0:T(4,128)(2,1)}), bf16[64,3,2048]{2,1,0:T(4,128)(2,1)}, u32[]{:S(2)}, u32[]{:S(2)}) async-start(bf16[64,3,2048]{2,1,0:T(4,128)(2,1)} %reshape.734), calls=%async_computation.8 | async-start | bytes 2097152 | tf_op jit(solution)/shard_map/all_to_all | solution.py:53
  321.7 11.8 collective-permute-start.2
  324.2 20.9 %all-to-all-start.9 = ((bf16[64,3,1]{1,2,0:T(2,128)(2,1)}), bf16[64,3,1]{1,2,0:T(2,128)(2,1)S(1)}, u32[]{:S(2)}, u32[]{:S(2)}) async-start(bf16[64,3,1]{1,2,0:T(2,128)(2,1)} %copy.226), calls=%async_computation.9 | async-start | bytes 65536 | tf_op jit(solution)/shard_map/all_to_all | solution.py:47
  345.1 32.7 %all-to-all-start.10 = ((bf16[64,3,2048]{2,1,0:T(4,128)(2,1)}), bf16[64,3,2048]{2,1,0:T(4,128)(2,1)}, u32[]{:S(2)}, u32[]{:S(2)}) async-start(bf16[64,3,2048]{2,1,0:T(4,128)(2,1)} %copy.227), calls=%async_computation.10 | async-start | bytes 2097152 | tf_op jit(solution)/shard_map/all_to_all | solution.py:46
  386.9 12.6 copy-start.23
  390.2 31.1 %all-to-all-start.11 = ((bf16[64,3,2048]{2,1,0:T(4,128)(2,1)}), bf16[64,3,2048]{2,1,0:T(4,128)(2,1)}, u32[]{:S(2)}, u32[]{:S(2)}) async-start(bf16[64,3,2048]{2,1,0:T(4,128)(2,1)} %reshape.736), calls=%async_computation.11 | async-start | bytes 2097152 | tf_op jit(solution)/shard_map/all_to_all | solution.py:53
  424.2 11.2 collective-permute-start.3
  426.2 20.7 %all-to-all-start.12 = ((bf16[64,3,1]{1,2,0:T(2,128)(2,1)}), bf16[64,3,1]{1,2,0:T(2,128)(2,1)S(1)}, u32[]{:S(2)}, u32[]{:S(2)}) async-start(bf16[64,3,1]{1,2,0:T(2,128)(2,1)} %copy.230), calls=%async_computation.12 | async-start | bytes 65536 | tf_op jit(solution)/shard_map/all_to_all | solution.py:47
  447.0 27.6 %all-to-all-start.13 = ((bf16[64,3,2048]{2,1,0:T(4,128)(2,1)}), bf16[64,3,2048]{2,1,0:T(4,128)(2,1)}, u32[]{:S(2)}, u32[]{:S(2)}) async-start(bf16[64,3,2048]{2,1,0:T(4,128)(2,1)} %copy.231), calls=%async_computation.13 | async-start | bytes 2097152 | tf_op jit(solution)/shard_map/all_to_all | solution.py:46
  476.6 8.9 copy-start.22
  479.9 30.7 %all-to-all-start.14 = ((bf16[64,3,2048]{2,1,0:T(4,128)(2,1)}), bf16[64,3,2048]{2,1,0:T(4,128)(2,1)}, u32[]{:S(2)}, u32[]{:S(2)}) async-start(bf16[64,3,2048]{2,1,0:T(4,128)(2,1)} %reshape.738), calls=%async_computation.14 | async-start | bytes 2097152 | tf_op jit(solution)/shard_map/all_to_all | solution.py:53
  513.5 11.1 collective-permute-start.4
  517.5 18.8 %all-to-all-start.15 = ((bf16[64,3,1]{1,2,0:T(2,128)(2,1)}), bf16[64,3,1]{1,2,0:T(2,128)(2,1)S(1)}, u32[]{:S(2)}, u32[]{:S(2)}) async-start(bf16[64,3,1]{1,2,0:T(2,128)(2,1)} %copy.234), calls=%async_computation.15 | async-start | bytes 65536 | tf_op jit(solution)/shard_map/all_to_all | solution.py:47
  536.3 28.2 %all-to-all-start.16 = ((bf16[64,3,2048]{2,1,0:T(4,128)(2,1)}), bf16[64,3,2048]{2,1,0:T(4,128)(2,1)}, u32[]{:S(2)}, u32[]{:S(2)}) async-start(bf16[64,3,2048]{2,1,0:T(4,128)(2,1)} %copy.235), calls=%async_computation.16 | async-start | bytes 2097152 | tf_op jit(solution)/shard_map/all_to_all | solution.py:46
  566.4 12.6 copy-start.21
  569.6 37.7 %all-to-all-start.17 = ((bf16[64,3,2048]{2,1,0:T(4,128)(2,1)}), bf16[64,3,2048]{2,1,0:T(4,128)(2,1)}, u32[]{:S(2)}, u32[]{:S(2)}) async-start(bf16[64,3,2048]{2,1,0:T(4,128)(2,1)} %reshape.740), calls=%async_computation.17 | async-start | bytes 2097152 | tf_op jit(solution)/shard_map/all_to_all | solution.py:53
  610.2 9.8 collective-permute-start.5
  612.5 19.1 %all-to-all-start.18 = ((bf16[64,3,1]{1,2,0:T(2,128)(2,1)}), bf16[64,3,1]{1,2,0:T(2,128)(2,1)S(1)}, u32[]{:S(2)}, u32[]{:S(2)}) async-start(bf16[64,3,1]{1,2,0:T(2,128)(2,1)} %copy.238), calls=%async_computation.18 | async-start | bytes 65536 | tf_op jit(solution)/shard_map/all_to_all | solution.py:47
  631.6 34.4 %all-to-all-start.19 = ((bf16[64,3,2048]{2,1,0:T(4,128)(2,1)}), bf16[64,3,2048]{2,1,0:T(4,128)(2,1)}, u32[]{:S(2)}, u32[]{:S(2)}) async-start(bf16[64,3,2048]{2,1,0:T(4,128)(2,1)} %copy.239), calls=%async_computation.19 | async-start | bytes 2097152 | tf_op jit(solution)/shard_map/all_to_all | solution.py:46
  666.0 24.4 %all-to-all-start.21 = ((bf16[64,3,2048]{2,1,0:T(4,128)(2,1)}), bf16[64,3,2048]{2,1,0:T(4,128)(2,1)}, u32[]{:S(2)}, u32[]{:S(2)}) async-start(bf16[64,3,2048]{2,1,0:T(4,128)(2,1)} %copy.242), calls=%async_computation.21 | async-start | bytes 2097152 | tf_op jit(solution)/shard_map/all_to_all | solution.py:57
  691.4 9.1 copy-start.20
  694.6 27.6 %copy-start.14 = (s32[64,32]{0,1:T(8,128)S(1)}, s32[64,32]{0,1:T(8,128)}, u32[]{:S(2)}) copy-start(s32[64,32]{0,1:T(8,128)} %copy-done.13) | copy-start | bytes 24580
  694.6 27.6 %all-to-all-start.22 = ((bf16[64,3,2048]{2,1,0:T(4,128)(2,1)}), bf16[64,3,2048]{2,1,0:T(4,128)(2,1)}, u32[]{:S(2)}, u32[]{:S(2)}) async-start(bf16[64,3,2048]{2,1,0:T(4,128)(2,1)} %reshape.745), calls=%async_computation.22 | async-start | bytes 2097152 | tf_op jit(solution)/shard_map/all_to_all | solution.py:61
  726.8 15.7 %collective-permute-start.6 = (bf16[32,2048]{1,0:T(8,128)(2,1)S(1)}, bf16[32,2048]{1,0:T(8,128)(2,1)S(1)}, u32[]{:S(2)}, u32[]{:S(2)}) collective-permute-start(bf16[32,2048]{1,0:T(8,128)(2,1)S(1)} %get-tuple-element.790), channel_id=1, source_target_pairs={{8,0},{16,8},{24,16},{9,1},{17,9},{25,17},{10,2},{18,10},{26,18},{... | collective-permute-start | bytes 393224 | tf_op jit(solution)/shard_map/ppermute | solution.py:14
  744.6 34.2 %all-to-all-start.23 = ((bf16[64,3,2048]{2,1,0:T(4,128)(2,1)}), bf16[64,3,2048]{2,1,0:T(4,128)(2,1)}, u32[]{:S(2)}, u32[]{:S(2)}) async-start(bf16[64,3,2048]{2,1,0:T(4,128)(2,1)} %copy.251), calls=%async_computation.23 | async-start | bytes 2097152 | tf_op jit(solution)/shard_map/all_to_all | solution.py:57
  783.1 24.3 %all-to-all-start.24 = ((bf16[64,3,2048]{2,1,0:T(4,128)(2,1)}), bf16[64,3,2048]{2,1,0:T(4,128)(2,1)}, u32[]{:S(2)}, u32[]{:S(2)}) async-start(bf16[64,3,2048]{2,1,0:T(4,128)(2,1)} %reshape.747), calls=%async_computation.24 | async-start | bytes 2097152 | tf_op jit(solution)/shard_map/all_to_all | solution.py:61
  811.5 12.8 collective-permute-start.7
  827.4 40.7 %all-to-all-start.25 = ((bf16[64,3,2048]{2,1,0:T(4,128)(2,1)}), bf16[64,3,2048]{2,1,0:T(4,128)(2,1)}, u32[]{:S(2)}, u32[]{:S(2)}) async-start(bf16[64,3,2048]{2,1,0:T(4,128)(2,1)} %copy.253), calls=%async_computation.25 | async-start | bytes 2097152 | tf_op jit(solution)/shard_map/all_to_all | solution.py:57
  869.2 8.4 copy-start.18
  872.5 24.3 %all-to-all-start.26 = ((bf16[64,3,2048]{2,1,0:T(4,128)(2,1)}), bf16[64,3,2048]{2,1,0:T(4,128)(2,1)}, u32[]{:S(2)}, u32[]{:S(2)}) async-start(bf16[64,3,2048]{2,1,0:T(4,128)(2,1)} %reshape.749), calls=%async_computation.26 | async-start | bytes 2097152 | tf_op jit(solution)/shard_map/all_to_all | solution.py:61
  900.9 18.4 %collective-permute-start.8 = (bf16[32,2048]{1,0:T(8,128)(2,1)S(1)}, bf16[32,2048]{1,0:T(8,128)(2,1)S(1)}, u32[]{:S(2)}, u32[]{:S(2)}) collective-permute-start(bf16[32,2048]{1,0:T(8,128)(2,1)S(1)} %get-tuple-element.786), channel_id=1, source_target_pairs={{8,0},{16,8},{24,16},{9,1},{17,9},{25,17},{10,2},{18,10},{26,18},{... | collective-permute-start | bytes 393224 | tf_op jit(solution)/shard_map/ppermute | solution.py:14
  922.4 36.3 %all-to-all-start.27 = ((bf16[64,3,2048]{2,1,0:T(4,128)(2,1)}), bf16[64,3,2048]{2,1,0:T(4,128)(2,1)}, u32[]{:S(2)}, u32[]{:S(2)}) async-start(bf16[64,3,2048]{2,1,0:T(4,128)(2,1)} %copy.255), calls=%async_computation.27 | async-start | bytes 2097152 | tf_op jit(solution)/shard_map/all_to_all | solution.py:57
  968.3 8.4 copy-start.17
  971.6 24.4 %all-to-all-start.28 = ((bf16[64,3,2048]{2,1,0:T(4,128)(2,1)}), bf16[64,3,2048]{2,1,0:T(4,128)(2,1)}, u32[]{:S(2)}, u32[]{:S(2)}) async-start(bf16[64,3,2048]{2,1,0:T(4,128)(2,1)} %reshape.751), calls=%async_computation.28 | async-start | bytes 2097152 | tf_op jit(solution)/shard_map/all_to_all | solution.py:61
  1000.1 9.3 collective-permute-start.9
  1012.4 36.3 %all-to-all-start.29 = ((bf16[64,3,2048]{2,1,0:T(4,128)(2,1)}), bf16[64,3,2048]{2,1,0:T(4,128)(2,1)}, u32[]{:S(2)}, u32[]{:S(2)}) async-start(bf16[64,3,2048]{2,1,0:T(4,128)(2,1)} %copy.257), calls=%async_computation.29 | async-start | bytes 2097152 | tf_op jit(solution)/shard_map/all_to_all | solution.py:57
  1058.4 8.4 copy-start.16
  1058.4 8.5 copy-start.27
  1061.6 24.4 %all-to-all-start.30 = ((bf16[64,3,2048]{2,1,0:T(4,128)(2,1)}), bf16[64,3,2048]{2,1,0:T(4,128)(2,1)}, u32[]{:S(2)}, u32[]{:S(2)}) async-start(bf16[64,3,2048]{2,1,0:T(4,128)(2,1)} %reshape.753), calls=%async_computation.30 | async-start | bytes 2097152 | tf_op jit(solution)/shard_map/all_to_all | solution.py:61
  1090.1 24.7 %collective-permute-start.10 = (bf16[32,2048]{1,0:T(8,128)(2,1)S(1)}, bf16[32,2048]{1,0:T(8,128)(2,1)S(1)}, u32[]{:S(2)}, u32[]{:S(2)}) collective-permute-start(bf16[32,2048]{1,0:T(8,128)(2,1)S(1)} %get-tuple-element.782), channel_id=1, source_target_pairs={{8,0},{16,8},{24,16},{9,1},{17,9},{25,17},{10,2},{18,10},{26,18},{... | collective-permute-start | bytes 393224 | tf_op jit(solution)/shard_map/ppermute | solution.py:14
  1117.9 33.7 %all-to-all-start.31 = ((bf16[64,3,2048]{2,1,0:T(4,128)(2,1)}), bf16[64,3,2048]{2,1,0:T(4,128)(2,1)}, u32[]{:S(2)}, u32[]{:S(2)}) async-start(bf16[64,3,2048]{2,1,0:T(4,128)(2,1)} %copy.259), calls=%async_computation.31 | async-start | bytes 2097152 | tf_op jit(solution)/shard_map/all_to_all | solution.py:57
  1161.3 8.8 copy-start.15
  1161.3 8.9 copy-start.26
  1164.6 33.5 %all-to-all-start.32 = ((bf16[64,3,2048]{2,1,0:T(4,128)(2,1)}), bf16[64,3,2048]{2,1,0:T(4,128)(2,1)}, u32[]{:S(2)}, u32[]{:S(2)}) async-start(bf16[64,3,2048]{2,1,0:T(4,128)(2,1)} %reshape.755), calls=%async_computation.32 | async-start | bytes 2097152 | tf_op jit(solution)/shard_map/all_to_all | solution.py:61
  1202.1 6.4 collective-permute-start.11
  1211.5 31.9 %all-to-all-start.33 = ((bf16[64,3,2048]{2,1,0:T(4,128)(2,1)}), bf16[64,3,2048]{2,1,0:T(4,128)(2,1)}, u32[]{:S(2)}, u32[]{:S(2)}) async-start(bf16[64,3,2048]{2,1,0:T(4,128)(2,1)} %copy.261), calls=%async_computation.33 | async-start | bytes 2097152 | tf_op jit(solution)/shard_map/all_to_all | solution.py:57
  1243.3 29.7 %all-to-all-start.20 = ((bf16[64,3,2048]{2,1,0:T(4,128)(2,1)}), bf16[64,3,2048]{2,1,0:T(4,128)(2,1)}, u32[]{:S(2)}, u32[]{:S(2)}) async-start(bf16[64,3,2048]{2,1,0:T(4,128)(2,1)} %reshape.742), calls=%async_computation.20 | async-start | bytes 2097152 | tf_op jit(solution)/shard_map/all_to_all | solution.py:53
  1261.1 17.2 %copy-start.6 = (bf16[5,32,2048]{2,1,0:T(8,128)(2,1)S(1)}, bf16[5,32,2048]{2,1,0:T(8,128)(2,1)}, u32[]{:S(2)}) copy-start(bf16[5,32,2048]{2,1,0:T(8,128)(2,1)} %get-tuple-element.848) | copy-start | bytes 1966084
  1273.1 27.3 %all-to-all-start.34 = ((bf16[64,3,2048]{2,1,0:T(4,128)(2,1)}), bf16[64,3,2048]{2,1,0:T(4,128)(2,1)S(1)}, u32[]{:S(2)}, u32[]{:S(2)}) async-start(bf16[64,3,2048]{2,1,0:T(4,128)(2,1)} %reshape.757), calls=%async_computation.34 | async-start | bytes 2097152 | tf_op jit(solution)/shard_map/all_to_all | solution.py:61
  1281.4 133.1 %copy-start.4 = (bf16[5,32,2048]{2,1,0:T(8,128)(2,1)S(1)}, bf16[5,32,2048]{2,1,0:T(8,128)(2,1)}, u32[]{:S(2)}) copy-start(bf16[5,32,2048]{2,1,0:T(8,128)(2,1)} %get-tuple-element.779) | copy-start | bytes 1966084
  (11 other events, 21.6 us)
